TPU v7x, 32 devices: a whole 2x2x4 slice. The times are simulated.
32 devices in a mesh: coil: 4 (over x, core), slab: 8 (over z, y).
Axes of the slice: x: 2, y: 2, z: 4, core: 2. Of those that a mesh axis runs over, the one named last changes fastest.
Arguments:
- kspace: bfloat16 [2, 8, 2, 32, 384, 128], P(None, 'coil', None, None, 'slab'), may hold values from -6 to 6
- coil_maps: bfloat16 [2, 8, 32, 384, 384], P(None, 'coil', None, 'slab'), may hold values from -1.1953125 to 1.1953125
- line_index: int32 [2, 384, 128], P(None, 'slab'), may hold values from 0 to 383, as said below
Outputs:
- harmonic_image: float32 [32, 2, 384, 384], P('coil', None, 'slab')
Inputs may be any that keep to these rules, and one draw needn't show every extreme that they name: `line_index`: for each phase offset and kz plane the 128 ky indices are distinct.
All inputs are finite; a program needn't handle non-finite values.
Results may differ from a plain program's by a relative error of at most 0.0043.
Values may be sent and summed in bfloat16 or wider, within the bound.
A program may use at most 64 MiB of HBM per device.

v0:
```python
import math

import jax
import jax.numpy as jnp
from jax import lax
from jax.sharding import PartitionSpec as P

NY = 384
NZ = 384
PHASES = 8


def line_tables(line_index, length):
    positions = lax.broadcasted_iota(jnp.int32, (1, 1, 1, length), 3)
    turn_count = line_index[..., None] * positions % length
    angles = turn_count.astype(jnp.float32) * (2.0 * math.pi / length)
    scaling = 1.0 / math.sqrt(length)
    return (
        (jnp.cos(angles) * scaling).astype(jnp.bfloat16),
        (jnp.sin(angles) * scaling).astype(jnp.bfloat16),
    )


def dense_tables(length):
    row_pos = lax.broadcasted_iota(jnp.int32, (length, length), 0)
    col_pos = lax.broadcasted_iota(jnp.int32, (length, length), 1)
    turn_count = row_pos * col_pos % length
    angles = turn_count.astype(jnp.float32) * (2.0 * math.pi / length)
    scaling = 1.0 / math.sqrt(length)
    return (
        (jnp.cos(angles) * scaling).astype(jnp.bfloat16),
        (jnp.sin(angles) * scaling).astype(jnp.bfloat16),
    )


def fold_offsets(real_part, imag_part, fold_axis):
    sum_real = None
    sum_imag = None
    for offset in range(real_part.shape[fold_axis]):
        phase_angle = 2.0 * math.pi * offset / PHASES
        cosine = math.cos(phase_angle)
        sine = math.sin(phase_angle)
        here_real = jnp.take(real_part, offset, axis=fold_axis)
        here_imag = jnp.take(imag_part, offset, axis=fold_axis)
        term_real = cosine * here_real + sine * here_imag
        term_imag = cosine * here_imag - sine * here_real
        if sum_real is None:
            sum_real, sum_imag = (term_real, term_imag)
        else:
            sum_real, sum_imag = (sum_real + term_real, sum_imag + term_imag)
    return jnp.stack([sum_real, sum_imag]).astype(jnp.bfloat16)


def lines_to_rows(left, right):
    return jnp.einsum("ctxkl,tkly->ctxky", left, right, preferred_element_type=jnp.float32)


def depth_pass(harmonic, depth_cos, depth_sin):

    def along(left, right):
        return jnp.einsum("cxky,kz->cxyz", left, right, preferred_element_type=jnp.float32)

    image_real = along(harmonic[0], depth_cos) - along(harmonic[1], depth_sin)
    image_imag = along(harmonic[0], depth_sin) + along(harmonic[1], depth_cos)
    return jnp.stack([image_real, image_imag])


def combine_coils(image, maps):
    add_real = jnp.sum(maps[0] * image[0] + maps[1] * image[1], axis=0)
    add_imag = jnp.sum(maps[0] * image[1] - maps[1] * image[0], axis=0)
    return jnp.stack([add_real, add_imag], axis=1)


def local(kspace, coil_maps, line_index):
    line_cos, line_sin = line_tables(line_index, NY)
    sample_real = kspace[0]
    sample_imag = kspace[1]
    hybrid_real = lines_to_rows(sample_real, line_cos) - lines_to_rows(sample_imag, line_sin)
    hybrid_imag = lines_to_rows(sample_real, line_sin) + lines_to_rows(sample_imag, line_cos)
    depth_cos, depth_sin = dense_tables(NZ)
    folded = fold_offsets(hybrid_real, hybrid_imag, 1)
    gathered = lax.all_to_all(folded, "slab", split_axis=4, concat_axis=3, tiled=True)
    maps = coil_maps.astype(jnp.float32)
    return lax.psum_scatter(
        combine_coils(depth_pass(gathered, depth_cos, depth_sin), maps),
        "coil",
        scatter_dimension=0,
        tiled=True,
    )


def solution(mesh):
    placed = (
        P(None, "coil", None, None, "slab", None),
        P(None, "coil", None, "slab", None),
        P(None, "slab", None),
    )
    return jax.shard_map(
        local, mesh=mesh, in_specs=placed, out_specs=P("coil", None, "slab", None), check_vma=False
    )
```

profile of v0, /device:TPU:0, one launch (start us, length us, event | category | flops | bytes accessed | tf_op | source)
XLA Modules:
  0.0 672.2 jit_solution(6098619045326092638)
XLA Ops:
  6.5 0.0 copy-start
  6.5 2.4 fusion.69
  9.0 0.0 copy-done
  9.0 93.6 %fusion.7 = f32[2,48,384,2,32]{2,4,3,1,0:T(8,128)S(1)} fusion(s32[2,48,128]{2,1,0:T(8,128)S(1)} %copy-done, bf16[1,2,2,32,48,128]{5,4,3,2,1,0:T(8,128)(2,1)S(1)} %get-tuple-element.35), kind=kOutput, calls=%fused_computation.14 | convolution fusion | flops 655884288 | bytes 11059200 | tf_op jit(solution)/shard_map/ctxkl,tkly->ctxky/dot_general | solution.py:55
  102.6 93.6 %fusion.9 = f32[2,48,384,2,32]{2,4,3,1,0:T(8,128)S(1)} fusion(s32[2,48,128]{2,1,0:T(8,128)S(1)} %copy-done, bf16[1,2,2,32,48,128]{5,4,3,2,1,0:T(8,128)(2,1)S(1)} %get-tuple-element.36), kind=kOutput, calls=%fused_computation.15 | convolution fusion | flops 655884288 | bytes 11059200 | tf_op jit(solution)/shard_map/ctxkl,tkly->ctxky/dot_general | solution.py:55
  196.2 93.5 %add_bitcast_fusion = f32[2,2,32,48,384]{4,2,0,3,1:T(8,128)S(1)} fusion(f32[2,48,384,2,32]{2,4,3,1,0:T(8,128)S(1)} %fusion.7, s32[2,48,128]{2,1,0:T(8,128)S(1)} %copy-done, bf16[1,2,2,32,48,128]{5,4,3,2,1,0:T(8,128)(2,1)S(1)} %get-tuple-element.36), kind=kOutput, calls=%fused_computation.12 | convolution fusion | flops 658243584 | bytes 20496384 | tf_op jit(solution)/shard_map/ctxkl,tkly->ctxky/dot_general | solution.py:55
  289.7 93.5 %subtract_bitcast_fusion = f32[2,2,32,48,384]{4,2,0,3,1:T(8,128)S(1)} fusion(f32[2,48,384,2,32]{2,4,3,1,0:T(8,128)S(1)} %fusion.9, s32[2,48,128]{2,1,0:T(8,128)S(1)} %copy-done, bf16[1,2,2,32,48,128]{5,4,3,2,1,0:T(8,128)(2,1)S(1)} %get-tuple-element.35), kind=kOutput, calls=%fused_computation.13 | convolution fusion | flops 658243584 | bytes 20496384 | tf_op jit(solution)/shard_map/ctxkl,tkly->ctxky/dot_general | solution.py:55
  383.2 2.7 fusion.21
  385.9 2.6 pad_maximum_fusion
  388.5 22.2 %copy.14 = bf16[2,2,32,48,384]{3,2,1,0,4:T(8,128)(2,1)} copy(bf16[2,2,32,48,384]{4,2,1,3,0:T(8,128)(2,1)} %pad_maximum_fusion) | data formatting | bytes 9437184 | tf_op jit(solution)/shard_map/stack | solution.py:51
  410.6 20.3 %reshape.79 = bf16[8,2,147456]{2,1,0:T(2,128)(2,1)} reshape(bf16[384,2,2,32,48]{4,3,2,1,0:T(8,128)(2,1)} %bitcast.135) | data formatting | bytes 9437184
  430.9 7.3 %all-to-all-start = ((bf16[8,2,147456]{2,1,0:T(2,128)(2,1)}), bf16[8,2,147456]{2,1,0:T(2,128)(2,1)}, u32[]{:S(2)}, u32[]{:S(2)}) async-start(bf16[8,2,147456]{2,1,0:T(2,128)(2,1)} %reshape.79), calls=%async_computation | async-start | bytes 9437184 | tf_op jit(solution)/shard_map/all_to_all | solution.py:82
  438.3 0.0 reduce-scatter.2.cloned.1.call-start
  438.3 6.8 %convert_element_type.32 = f32[2,2,32,48,384]{4,3,2,1,0:T(8,128)} convert(bf16[2,2,32,48,384]{4,3,2,1,0:T(8,128)(2,1)} %param.8) | non-fusion elementwise | flops 2359296 | bytes 14155776 | tf_op jit(solution)/shard_map/convert_element_type | solution.py:83
  445.0 97.7 %all-to-all-done = bf16[8,2,147456]{2,1,0:T(2,128)(2,1)} async-done(((bf16[8,2,147456]{2,1,0:T(2,128)(2,1)}), bf16[8,2,147456]{2,1,0:T(2,128)(2,1)}, u32[]{:S(2)}, u32[]{:S(2)}) %all-to-all-start) | async-done | bytes 4718624 | tf_op jit(solution)/shard_map/all_to_all | solution.py:82
  542.8 14.1 %reshape.80 = bf16[384,2,2,32,48]{4,3,2,1,0:T(8,128)(2,1)} reshape(bf16[8,2,147456]{2,1,0:T(2,128)(2,1)} %all-to-all-done) | data formatting | bytes 9437184
  556.9 11.5 %copy.32 = bf16[2,2,32,48,8,48]{3,4,5,2,1,0:T(8,128)(2,1)S(1)} copy(bf16[2,2,32,48,8,48]{3,2,1,0,5,4:T(8,128)(2,1)} %bitcast.134) | data formatting | bytes 9437184 | tf_op jit(solution)/shard_map/all_to_all | solution.py:82
  568.4 5.6 fusion.68
  574.1 8.1 %squeeze.25 = bf16[2,32,384,48]{2,3,1,0:T(8,128)(2,1)S(1)} reshape(bf16[1,2,32,8,48,48]{4,3,5,2,1,0:T(8,128)(2,1)} %get-tuple-element.34) | data formatting | bytes 4718592 | tf_op jit(solution)/shard_map/squeeze | solution.py:63
  582.1 5.7 fusion.30
  587.8 5.6 fusion.34
  593.4 8.1 %squeeze.26 = bf16[2,32,384,48]{2,3,1,0:T(8,128)(2,1)S(1)} reshape(bf16[1,2,32,8,48,48]{4,3,5,2,1,0:T(8,128)(2,1)} %get-tuple-element.33) | data formatting | bytes 4718592 | tf_op jit(solution)/shard_map/squeeze | solution.py:63
  601.4 5.6 convolution_subtract_fusion
  607.0 8.7 %add_reduce_fusion = (f32[32,48,384]{2,1,0:T(8,128)S(1)}, f32[32,48,384]{2,1,0:T(8,128)S(1)}) fusion(f32[2,32,48,384]{3,2,1,0:T(8,128)S(1)} %convolution_subtract_fusion, f32[2,2,32,48,384]{4,3,2,1,0:T(8,128)} %convert_element_type.32, f32[2,32,48,384]{3,2,1,0:T(8,128)} %fusion.30, bf16[2,32,384,48]{2,3,1,0:T(8,128)(2,1)S(1)} %squeeze.26), kind=kOutput, calls=%fused_computation.29 | convolution fusion | flops 917028864 | bytes 25952256 | tf_op jit(solution)/shard_map/cxky,kz->cxyz/dot_general | solution.py:61
  615.7 2.5 pad_maximum_fusion.1
  618.2 0.0 reduce-scatter.2.cloned.1.call-update
  618.3 47.1 %reduce-scatter.2.cloned.1.call-done = f32[8,2,48,384]{3,2,1,0:T(8,128)} async-done(((f32[32,2,48,384]{3,2,1,0:T(8,128)}), f32[8,2,48,384]{3,2,1,0:T(8,128)}) %reduce-scatter.2.cloned.1.call-update) | async-done | bytes 1179664 | tf_op jit(solution)/shard_map/reduce_scatter | solution.py:84
Async XLA Ops:
  6.5 2.4 copy-start
  430.9 111.8 %all-to-all-start = ((bf16[8,2,147456]{2,1,0:T(2,128)(2,1)}), bf16[8,2,147456]{2,1,0:T(2,128)(2,1)}, u32[]{:S(2)}, u32[]{:S(2)}) async-start(bf16[8,2,147456]{2,1,0:T(2,128)(2,1)} %reshape.79), calls=%async_computation | async-start | bytes 9437184 | tf_op jit(solution)/shard_map/all_to_all | solution.py:82
  438.3 227.2 %reduce-scatter.2.cloned.1.call-start = ((), (), s32[]{:S(2)}) async-start(), calls=%async_computation.2 | async-start | bytes 5898240 | tf_op jit(solution)/shard_map/reduce_scatter | solution.py:84
Sparse Core Ops, SparseCore 0:
  618.4 46.9 reduce-scatter.1
where the time goes:
time: 673 us; the launch traced here: 672 us
  matrix products  400 us (59%)
  waiting for transfers between devices  145 us (22%)
  local copies, waits for them, and re-layouts  92.3 us (14%)
  other arithmetic  14.5 us (2%)
  between operations  13.5 us (2%)
  starting transfers between devices  7.35 us (1%)
    dot_general x4, matrix products, lines_to_rows(): jnp.einsum('ctxkl,tkly->ctxky', left, right, preferred_element_type=jnp.f...  374 us
    all_to_all x1, waiting for transfers between devices, local(): lax.all_to_all(folded, 'slab', split_axis=4, concat_axis=3, tiled=True)  97.7 us
    reduce_scatter x1, waiting for transfers between devices, local(): lax.psum_scatter(combine_coils(depth_pass(gathered, depth_cos, depth_sin)...  47.1 us
    unnamed x4, local copies, waits for them, and re-layouts  34.5 us
    dot_general x4, matrix products, along(): jnp.einsum('cxky,kz->cxyz', left, right, preferred_element_type=jnp.float32)  25.5 us
    another operation x1, local copies, waits for them, and re-layouts, fold_offsets(): return jnp.stack([sum_real, sum_imag]).astype(jnp.bfloat16)  22.2 us
    squeeze x2, local copies, waits for them, and re-layouts, depth_pass(): image_real = along(harmonic[0], depth_cos) - along(harmonic[1], depth_sin)  16.1 us
  transfers between devices with their start and end apart: 2, of which 2 were waited for; matrix products, arithmetic and copies ran while one was open for 1% of the time, Pallas kernels for 0%

commit v1 on v0

v1 whole, which is shorter than its diff:
```python
import functools
import math

import jax
import jax.numpy as jnp
import numpy as np
from jax import lax
from jax.experimental import pallas as pl
from jax.experimental.pallas import tpu as pltpu
from jax.sharding import PartitionSpec as P

PHASES = 8
LANES = 128
MESH = pl.DeviceIdType.MESH


def up(value, unit):
    return -(-value // unit) * unit


def dense_table(rows, row_ok, length):
    turns = rows[:, None].astype(np.int64) * np.arange(length)[None, :] % length
    angles = turns.astype(np.float64) * (2.0 * math.pi / length)
    scaling = row_ok[:, None] / math.sqrt(length)
    cos, sin = np.cos(angles) * scaling, np.sin(angles) * scaling
    return np.concatenate([cos, sin], 1), np.concatenate([-sin, cos], 1)


def kernel(
    dims,
    kspace_ref, maps_ref, index_ref, ky_ref, kz_ref, out_ref,
    raw, samples, grid, maps, send, recv, image, part_send, part_recv,
    in_sem, send_sem, recv_sem, own_sem, psend_sem, precv_sem,
):
    slab, coil, coils, offs, xr, kzb, kzp, lines, ny, yb, nz = dims
    me_s, me_c = lax.axis_index("slab"), lax.axis_index("coil")
    rows = 2 * coils * xr
    kzs = up(kzb, 8)
    chunks = xr // slab
    xo = xr // coil
    owners = slab // xo

    load_k = pltpu.make_async_copy(kspace_ref, raw, in_sem.at[0])
    load_k.start()
    load_m = pltpu.make_async_copy(maps_ref, maps, in_sem.at[1])
    load_m.start()

    barrier = pltpu.get_barrier_semaphore()
    for o in range(1, slab):
        pl.semaphore_signal(
            barrier, inc=1, device_id={"slab": lax.rem(me_s + o, slab)}, device_id_type=MESH
        )
    for o in range(1, coil):
        pl.semaphore_signal(
            barrier, inc=1, device_id={"coil": lax.rem(me_c + o, coil)}, device_id_type=MESH
        )

    if kzp != kzb:
        grid[...] = jnp.zeros_like(grid)
    load_k.wait()

    def unpack(x, carry):
        for c in range(coils):
            for t in range(offs):
                angle = 2.0 * math.pi * t / PHASES
                real = raw[0, c, t, x].astype(jnp.float32)
                imag = raw[1, c, t, x].astype(jnp.float32)
                if t:
                    cosine, sine = math.cos(angle), math.sin(angle)
                    real, imag = cosine * real + sine * imag, cosine * imag - sine * real
                for part, value in ((0, real), (1, imag)):
                    at = pl.multiple_of(((part * coils + c) * xr + x) * kzs, 8)
                    samples[t, pl.ds(at, kzb), :] = value
        return carry

    lax.fori_loop(0, xr, unpack, 0)

    ky_at = lax.broadcasted_iota(jnp.int32, (ny, offs * lines), 0)

    def place(kz, carry):
        picked = jnp.concatenate([index_ref[t, pl.ds(kz, 1), :] for t in range(offs)], axis=1)
        hot = jnp.where(ky_at == picked, 1.0, 0.0).astype(jnp.bfloat16)
        left = jnp.concatenate(
            [samples[t, pl.ds(kz, rows, stride=kzs), :].astype(jnp.bfloat16) for t in range(offs)],
            axis=1,
        )
        grid_at = pl.multiple_of(kz * rows, 8)
        placed = lax.dot_general(
            left, hot, (((1,), (1,)), ((), ())), preferred_element_type=jnp.float32
        )
        for j in range(ny // LANES):
            grid[j, pl.ds(grid_at, rows), :] = placed[:, j * LANES : (j + 1) * LANES]
        return carry

    lax.fori_loop(0, kzb, place, 0)

    pl.semaphore_wait(barrier, slab + coil - 2)

    def chunk_of(k):
        return lax.rem(lax.div(me_c, owners) + 1 + k, chunks)

    def send_copy(k, c, o):
        return pltpu.make_async_remote_copy(
            src_ref=send.at[k, c, lax.rem(me_s + o, slab)],
            dst_ref=recv.at[k, c, me_s],
            send_sem=send_sem.at[k, c, o],
            recv_sem=recv_sem.at[k, c, o],
            device_id={"slab": lax.rem(me_s + o, slab)},
            device_id_type=MESH,
        )

    def recv_copy(k, c, o):
        return pltpu.make_async_remote_copy(
            src_ref=send.at[k, c, lax.rem(me_s + o, slab)],
            dst_ref=recv.at[k, c, lax.rem(me_s + slab - o, slab)],
            send_sem=send_sem.at[k, c, o],
            recv_sem=recv_sem.at[k, c, o],
            device_id={"slab": lax.rem(me_s + o, slab)},
            device_id_type=MESH,
        )

    def own_copy(k, c):
        return pltpu.make_async_copy(send.at[k, c, me_s], recv.at[k, c, me_s], own_sem.at[k, c])

    lane = lax.broadcasted_iota(jnp.int32, (kzp, LANES), 1)

    def rows_pass(step, carry):
        k, c = lax.div(step, coils), lax.rem(step, coils)
        first = chunk_of(k) * slab
        lefts = []
        for i in range(slab):
            pieces = []
            for part in range(2):
                at = (part * coils + c) * xr + first + i
                for j in range(ny // LANES):
                    pieces.append(grid[j, pl.ds(at, kzp, stride=rows), :].astype(jnp.bfloat16))
            lefts.append(jnp.concatenate(pieces, axis=1))
        hybrid = jnp.dot(
            jnp.concatenate(lefts, axis=0), ky_ref[...], preferred_element_type=jnp.float32
        )
        for part in range(2):
            turned = []
            for i in range(slab):
                value = hybrid[i * kzp : (i + 1) * kzp, part * ny : (part + 1) * ny]
                turned.append(pltpu.roll(value, i * yb, 1) if i else value)
            for d in range(slab):
                for j in range(ny // LANES):
                    low, high = j * LANES // yb, ((j + 1) * LANES - 1) // yb
                    cut = slice(j * LANES, (j + 1) * LANES)
                    tile = turned[(low - d) % slab][:, cut]
                    for p in range(low + 1, high + 1):
                        tile = jnp.where(
                            lane >= p * yb - j * LANES, turned[(p - d) % slab][:, cut], tile
                        )
                    send[k, c, d, part, :, cut] = tile.astype(jnp.bfloat16)
        for o in range(1, slab):
            send_copy(k, c, o).start()
        own_copy(k, c).start()
        return carry

    lax.fori_loop(0, chunks * coils, rows_pass, 0)
    load_m.wait()

    def part_copy(k, q):
        owner = chunk_of(k) * owners + q
        return pltpu.make_async_remote_copy(
            src_ref=part_send.at[chunk_of(k), pl.ds(q * xo, xo)],
            dst_ref=part_recv.at[lax.rem(owner - me_c + coil, coil)],
            send_sem=psend_sem.at[k, q],
            recv_sem=precv_sem.at[lax.rem(owner - me_c + coil, coil)],
            device_id={"coil": owner},
            device_id_type=MESH,
        )

    def depth_pass(k, carry):
        first = chunk_of(k) * slab

        def one_coil(c, inner):
            own_copy(k, c).wait()
            for o in range(1, slab):
                recv_copy(k, c, o).wait_recv()
            block = recv[k, c].reshape(slab * 2 * kzp, slab * yb)
            image[c] = lax.dot_general(
                block, kz_ref[...], (((0,), (0,)), ((), ())), preferred_element_type=jnp.float32
            )
            return inner

        lax.fori_loop(0, coils, one_coil, 0)
        for p in range(slab):
            x = lax.rem(p - me_s + slab, slab)
            add_real = add_imag = None
            for c in range(coils):
                real = image[c, p * yb : (p + 1) * yb, :nz]
                imag = image[c, p * yb : (p + 1) * yb, nz:]
                map_real = maps[0, c, first + x].astype(jnp.float32)
                map_imag = maps[1, c, first + x].astype(jnp.float32)
                term_real = map_real * real + map_imag * imag
                term_imag = map_real * imag - map_imag * real
                add_real = term_real if add_real is None else add_real + term_real
                add_imag = term_imag if add_imag is None else add_imag + term_imag
            part_send[chunk_of(k), x, 0] = add_real.astype(jnp.bfloat16)
            part_send[chunk_of(k), x, 1] = add_imag.astype(jnp.bfloat16)
        for q in range(owners):
            @pl.when(chunk_of(k) * owners + q != me_c)
            def _():
                part_copy(k, q).start()
        return carry

    lax.fori_loop(0, chunks, depth_pass, 0)

    for o in range(1, coil):
        pltpu.make_async_remote_copy(
            src_ref=part_recv.at[o],
            dst_ref=part_recv.at[o],
            send_sem=psend_sem.at[0, 0],
            recv_sem=precv_sem.at[o],
            device_id={"coil": lax.rem(me_c + o, coil)},
            device_id_type=MESH,
        ).wait_recv()
    own_chunk, own_at = lax.div(me_c, owners), lax.rem(me_c, owners) * xo

    def total(i, carry):
        value = part_send[own_chunk, own_at + i].astype(jnp.float32)
        for o in range(1, coil):
            value = value + part_recv[o, i].astype(jnp.float32)
        out_ref[i] = value
        return carry

    lax.fori_loop(0, xo, total, 0)

    def drain(k, carry):
        for c in range(coils):
            for o in range(1, slab):
                send_copy(k, c, o).wait_send()
        for q in range(owners):
            @pl.when(chunk_of(k) * owners + q != me_c)
            def _():
                part_copy(k, q).wait_send()
        return carry

    lax.fori_loop(0, chunks, drain, 0)


def local(mesh, kspace, coil_maps, line_index):
    slab, coil = mesh.shape["slab"], mesh.shape["coil"]
    _, coils, offs, xr, kzb, lines = kspace.shape
    yb, nz = coil_maps.shape[3:]
    ny = yb * slab
    kzp = up(kzb, 16)
    dims = (slab, coil, coils, offs, xr, kzb, kzp, lines, ny, yb, nz)
    chunks, xo = xr // slab, xr // coil
    owners = slab // xo
    rows = 2 * coils * xr
    f32, bf16 = jnp.float32, jnp.bfloat16

    ky_table = np.concatenate(dense_table(np.arange(ny), np.ones(ny), ny), 0)
    local_kz = np.arange(kzp)
    per_slab = []
    for s in range(slab):
        per_slab += dense_table(s * kzb + local_kz, (local_kz < kzb) * 1.0, nz)
    kz_table = np.concatenate(per_slab, 0)
    ky_table = jnp.asarray(ky_table.astype(np.float32)).astype(bf16)
    kz_table = jnp.asarray(kz_table.astype(np.float32)).astype(bf16)

    vmem, anywhere = pl.BlockSpec(memory_space=pltpu.VMEM), pl.BlockSpec(memory_space=pl.ANY)
    dma = pltpu.SemaphoreType.DMA
    return pl.pallas_call(
        functools.partial(kernel, dims),
        out_shape=jax.ShapeDtypeStruct((xo, 2, yb, nz), f32),
        in_specs=[anywhere, anywhere, vmem, vmem, vmem],
        out_specs=vmem,
        scratch_shapes=[
            pltpu.VMEM(kspace.shape, bf16),
            pltpu.VMEM((offs, rows * up(kzb, 8), lines), f32),
            pltpu.VMEM((ny // LANES, kzp * rows, LANES), f32),
            pltpu.VMEM(coil_maps.shape, bf16),
            pltpu.VMEM((chunks, coils, slab, 2, kzp, ny), bf16),
            pltpu.VMEM((chunks, coils, slab, 2, kzp, ny), bf16),
            pltpu.VMEM((coils, ny, 2 * nz), f32),
            pltpu.VMEM((chunks, slab, 2, yb, nz), bf16),
            pltpu.VMEM((coil, xo, 2, yb, nz), bf16),
            dma((2,)),
            dma((chunks, coils, slab)),
            dma((chunks, coils, slab)),
            dma((chunks, coils)),
            dma((chunks, owners)),
            dma((coil,)),
        ],
        compiler_params=pltpu.CompilerParams(
            collective_id=0, has_side_effects=True, vmem_limit_bytes=63 * 1024 * 1024
        ),
    )(kspace, coil_maps, line_index, ky_table, kz_table)


def solution(mesh):
    placed = (
        P(None, "coil", None, None, "slab", None),
        P(None, "coil", None, "slab", None),
        P(None, "slab", None),
    )
    return jax.shard_map(
        functools.partial(local, mesh),
        mesh=mesh,
        in_specs=placed,
        out_specs=P("coil", None, "slab", None),
        check_vma=False,
    )
```

time: 673 us -> 126 us (0.19)
  matrix products: 400 us -> 0 us
  waiting for transfers between devices: 145 us -> 0 us
  Pallas kernels: 0 us -> 123 us
  local copies, waits for them, and re-layouts: 92.3 us -> 2.37 us
  other arithmetic: 14.5 us -> 0 us
  between operations: 13.5 us -> 0.01 us
  starting transfers between devices: 7.35 us -> 0 us
    dot_general x8 -> x0, matrix products: 400 us -> none  [the longest x4 374 us: lines_to_rows(): jnp.einsum('ctxkl,tkly->ctxky', left, right, preferred_element_type=jnp.f...]
    pallas_call x0 -> x1, Pallas kernels: none -> 123 us  [local(): pl.pallas_call(functools.partial(kernel, dims), out_shape=jax.ShapeDtypeS...]
    all_to_all x1 -> x0, waiting for transfers between devices: 97.7 us -> none  [local(): lax.all_to_all(folded, 'slab', split_axis=4, concat_axis=3, tiled=True)]
    reduce_scatter x1 -> x0, waiting for transfers between devices: 47.1 us -> none  [local(): lax.psum_scatter(combine_coils(depth_pass(gathered, depth_cos, depth_sin)...]
    unnamed x4 -> x1, local copies, waits for them, and re-layouts: 34.5 us -> 2.37 us
    another operation x1 -> x0, local copies, waits for them, and re-layouts: 22.2 us -> none  [fold_offsets(): return jnp.stack([sum_real, sum_imag]).astype(jnp.bfloat16)]
    squeeze x2 -> x0, local copies, waits for them, and re-layouts: 16.1 us -> none  [depth_pass(): image_real = along(harmonic[0], depth_cos) - along(harmonic[1], depth_sin)]
    all_to_all x1 -> x0, local copies, waits for them, and re-layouts: 11.5 us -> none  [local(): lax.all_to_all(folded, 'slab', split_axis=4, concat_axis=3, tiled=True)]
  transfers between devices with their start and end apart: 2 -> 0, of which waited for: 2 -> 0; matrix products, arithmetic and copies ran while one was open for 1% -> 0% of each run, Pallas kernels for 0% -> 0%
where the time goes in v1:
time: 126 us; the launch traced here: 125 us
  Pallas kernels  123 us (98%)
  local copies, waits for them, and re-layouts  2.37 us (2%)
    pallas_call x1, Pallas kernels, local(): pl.pallas_call(functools.partial(kernel, dims), out_shape=jax.ShapeDtypeS...  123 us

profile of v1, /device:TPU:0, one launch (start us, length us, event | category | flops | bytes accessed | tf_op | source)
XLA Modules:
  0.0 125.4 jit_solution(16517737017010442990)
XLA Ops:
  0.0 123.0 %shard_map.55 = f32[8,2,48,384]{3,2,1,0:T(8,128)} custom-call(bf16[2,2,2,32,48,128]{5,4,3,2,1,0:T(8,128)(2,1)} %kspace_ref.1, bf16[2,2,32,48,384]{4,3,2,1,0:T(8,128)(2,1)} %maps_ref.1, s32[2,48,128]{2,1,0:T(8,128)} %index_ref.1, bf16[768,768]{1,0:T(8,128)(2,1)} %constant.8.ky_ref, bf16[768,768]{1,0:T(8,128)(2,1)} %constant.9.kz_ref), custom_call_target="tpu_custom_call" | custom-call | tf_op jit(solution)/shard_map/pallas_call | solution.py:267
  123.1 2.4 %copy.7 = f32[8,2,48,384]{3,2,1,0:T(8,128)} copy(f32[8,2,48,384]{3,2,1,0:T(8,128)} %shard_map.55) | data formatting | bytes 2359296

commit v2 on v1

--- a/solution.py
+++ b/solution.py
@@ -11,7 +11,14 @@
 
 PHASES = 8
 LANES = 128
+UNROLL = 8
+VLIM = 52
+ROWS = 16
 MESH = pl.DeviceIdType.MESH
+
+
+def ORDER(slab):
+    return range(1, slab)
 
 
 def up(value, unit):
@@ -29,21 +36,17 @@
 def kernel(
     dims,
     kspace_ref, maps_ref, index_ref, ky_ref, kz_ref, out_ref,
-    raw, samples, grid, maps, send, recv, image, part_send, part_recv,
+    raw, samples, grid, maps, ky_tab, kz_tab, send, recv, image, part_send, part_recv,
     in_sem, send_sem, recv_sem, own_sem, psend_sem, precv_sem,
 ):
     slab, coil, coils, offs, xr, kzb, kzp, lines, ny, yb, nz = dims
     me_s, me_c = lax.axis_index("slab"), lax.axis_index("coil")
-    rows = 2 * coils * xr
+    rows = 2 * coils * slab
     kzs = up(kzb, 8)
     chunks = xr // slab
     xo = xr // coil
     owners = slab // xo
-
-    load_k = pltpu.make_async_copy(kspace_ref, raw, in_sem.at[0])
-    load_k.start()
-    load_m = pltpu.make_async_copy(maps_ref, maps, in_sem.at[1])
-    load_m.start()
+    blocks = kzp // ROWS
 
     barrier = pltpu.get_barrier_semaphore()
     for o in range(1, slab):
@@ -55,29 +58,34 @@
             barrier, inc=1, device_id={"coil": lax.rem(me_c + o, coil)}, device_id_type=MESH
         )
 
+    load_k = pltpu.make_async_copy(kspace_ref, raw, in_sem.at[0])
+    load_m = pltpu.make_async_copy(maps_ref, maps, in_sem.at[1])
+    load_y = pltpu.make_async_copy(ky_ref, ky_tab, in_sem.at[2])
+    load_z = pltpu.make_async_copy(kz_ref, kz_tab, in_sem.at[3])
+    for load in (load_k, load_y, load_m, load_z):
+        load.start()
+
     if kzp != kzb:
         grid[...] = jnp.zeros_like(grid)
-    load_k.wait()
-
-    def unpack(x, carry):
+
+    def unpack(first, i, carry):
         for c in range(coils):
             for t in range(offs):
                 angle = 2.0 * math.pi * t / PHASES
-                real = raw[0, c, t, x].astype(jnp.float32)
-                imag = raw[1, c, t, x].astype(jnp.float32)
+                real = raw[0, c, t, first + i].astype(jnp.float32)
+                imag = raw[1, c, t, first + i].astype(jnp.float32)
                 if t:
                     cosine, sine = math.cos(angle), math.sin(angle)
                     real, imag = cosine * real + sine * imag, cosine * imag - sine * real
                 for part, value in ((0, real), (1, imag)):
-                    at = pl.multiple_of(((part * coils + c) * xr + x) * kzs, 8)
+                    at = pl.multiple_of(((part * coils + c) * slab + i) * kzs, 8)
                     samples[t, pl.ds(at, kzb), :] = value
         return carry
 
-    lax.fori_loop(0, xr, unpack, 0)
-
     ky_at = lax.broadcasted_iota(jnp.int32, (ny, offs * lines), 0)
 
-    def place(kz, carry):
+    def place(first_kz, step, carry):
+        kz = first_kz + step
         picked = jnp.concatenate([index_ref[t, pl.ds(kz, 1), :] for t in range(offs)], axis=1)
         hot = jnp.where(ky_at == picked, 1.0, 0.0).astype(jnp.bfloat16)
         left = jnp.concatenate(
@@ -92,12 +100,19 @@
             grid[j, pl.ds(grid_at, rows), :] = placed[:, j * LANES : (j + 1) * LANES]
         return carry
 
-    lax.fori_loop(0, kzb, place, 0)
-
-    pl.semaphore_wait(barrier, slab + coil - 2)
 
     def chunk_of(k):
         return lax.rem(lax.div(me_c, owners) + 1 + k, chunks)
+
+    def block_copy(k, c, o, kz_at):
+        return pltpu.make_async_remote_copy(
+            src_ref=send.at[k, c, lax.rem(me_s + o, slab), :, pl.ds(kz_at, ROWS)],
+            dst_ref=recv.at[k, c, me_s, :, pl.ds(kz_at, ROWS)],
+            send_sem=send_sem.at[k, c, o],
+            recv_sem=recv_sem.at[k, c, o],
+            device_id={"slab": lax.rem(me_s + o, slab)},
+            device_id_type=MESH,
+        )
 
     def send_copy(k, c, o):
         return pltpu.make_async_remote_copy(
@@ -122,26 +137,26 @@
     def own_copy(k, c):
         return pltpu.make_async_copy(send.at[k, c, me_s], recv.at[k, c, me_s], own_sem.at[k, c])
 
-    lane = lax.broadcasted_iota(jnp.int32, (kzp, LANES), 1)
-
-    def rows_pass(step, carry):
-        k, c = lax.div(step, coils), lax.rem(step, coils)
-        first = chunk_of(k) * slab
+    lane = lax.broadcasted_iota(jnp.int32, (ROWS, LANES), 1)
+
+    def rows_pass(k, b, c, carry):
+        kz_at = pl.multiple_of(b * ROWS, ROWS)
         lefts = []
         for i in range(slab):
             pieces = []
             for part in range(2):
-                at = (part * coils + c) * xr + first + i
+                at = (part * coils + c) * slab + i
                 for j in range(ny // LANES):
-                    pieces.append(grid[j, pl.ds(at, kzp, stride=rows), :].astype(jnp.bfloat16))
+                    here = grid[j, pl.ds(kz_at * rows + at, ROWS, stride=rows), :]
+                    pieces.append(here.astype(jnp.bfloat16))
             lefts.append(jnp.concatenate(pieces, axis=1))
         hybrid = jnp.dot(
-            jnp.concatenate(lefts, axis=0), ky_ref[...], preferred_element_type=jnp.float32
+            jnp.concatenate(lefts, axis=0), ky_tab[...], preferred_element_type=jnp.float32
         )
         for part in range(2):
             turned = []
             for i in range(slab):
-                value = hybrid[i * kzp : (i + 1) * kzp, part * ny : (part + 1) * ny]
+                value = hybrid[i * ROWS : (i + 1) * ROWS, part * ny : (part + 1) * ny]
                 turned.append(pltpu.roll(value, i * yb, 1) if i else value)
             for d in range(slab):
                 for j in range(ny // LANES):
@@ -152,14 +167,33 @@
                         tile = jnp.where(
                             lane >= p * yb - j * LANES, turned[(p - d) % slab][:, cut], tile
                         )
-                    send[k, c, d, part, :, cut] = tile.astype(jnp.bfloat16)
-        for o in range(1, slab):
-            send_copy(k, c, o).start()
-        own_copy(k, c).start()
-        return carry
-
-    lax.fori_loop(0, chunks * coils, rows_pass, 0)
+                    send[k, c, d, part, pl.ds(kz_at, ROWS), cut] = tile.astype(jnp.bfloat16)
+        for o in ORDER(slab):
+            block_copy(k, c, o, kz_at).start()
+
+        @pl.when(b == blocks - 1)
+        def _():
+            own_copy(k, c).start()
+
+        return carry
+
+    def chunk_pass(k, carry):
+        first = chunk_of(k) * slab
+        lax.fori_loop(0, slab, functools.partial(unpack, first), 0)
+
+        def block_pass(b, inner):
+            count = min(ROWS, kzb)
+            lax.fori_loop(0, count, functools.partial(place, b * ROWS), 0, unroll=UNROLL)
+            return lax.fori_loop(0, coils, functools.partial(rows_pass, k, b), inner)
+
+        return lax.fori_loop(0, blocks, block_pass, carry)
+
+    load_k.wait()
+    load_y.wait()
+    pl.semaphore_wait(barrier, slab + coil - 2)
+    lax.fori_loop(0, chunks, chunk_pass, 0)
     load_m.wait()
+    load_z.wait()
 
     def part_copy(k, q):
         owner = chunk_of(k) * owners + q
@@ -181,7 +215,7 @@
                 recv_copy(k, c, o).wait_recv()
             block = recv[k, c].reshape(slab * 2 * kzp, slab * yb)
             image[c] = lax.dot_general(
-                block, kz_ref[...], (((0,), (0,)), ((), ())), preferred_element_type=jnp.float32
+                block, kz_tab[...], (((0,), (0,)), ((), ())), preferred_element_type=jnp.float32
             )
             return inner
 
@@ -250,7 +284,7 @@
     dims = (slab, coil, coils, offs, xr, kzb, kzp, lines, ny, yb, nz)
     chunks, xo = xr // slab, xr // coil
     owners = slab // xo
-    rows = 2 * coils * xr
+    rows = 2 * coils * slab
     f32, bf16 = jnp.float32, jnp.bfloat16
 
     ky_table = np.concatenate(dense_table(np.arange(ny), np.ones(ny), ny), 0)
@@ -262,24 +296,26 @@
     ky_table = jnp.asarray(ky_table.astype(np.float32)).astype(bf16)
     kz_table = jnp.asarray(kz_table.astype(np.float32)).astype(bf16)
 
-    vmem, anywhere = pl.BlockSpec(memory_space=pltpu.VMEM), pl.BlockSpec(memory_space=pl.ANY)
+    vmem, hbm = pl.BlockSpec(memory_space=pltpu.VMEM), pl.BlockSpec(memory_space=pltpu.HBM)
     dma = pltpu.SemaphoreType.DMA
     return pl.pallas_call(
         functools.partial(kernel, dims),
         out_shape=jax.ShapeDtypeStruct((xo, 2, yb, nz), f32),
-        in_specs=[anywhere, anywhere, vmem, vmem, vmem],
+        in_specs=[hbm, hbm, vmem, hbm, hbm],
         out_specs=vmem,
         scratch_shapes=[
             pltpu.VMEM(kspace.shape, bf16),
             pltpu.VMEM((offs, rows * up(kzb, 8), lines), f32),
             pltpu.VMEM((ny // LANES, kzp * rows, LANES), f32),
             pltpu.VMEM(coil_maps.shape, bf16),
+            pltpu.VMEM(ky_table.shape, bf16),
+            pltpu.VMEM(kz_table.shape, bf16),
             pltpu.VMEM((chunks, coils, slab, 2, kzp, ny), bf16),
             pltpu.VMEM((chunks, coils, slab, 2, kzp, ny), bf16),
             pltpu.VMEM((coils, ny, 2 * nz), f32),
             pltpu.VMEM((chunks, slab, 2, yb, nz), bf16),
             pltpu.VMEM((coil, xo, 2, yb, nz), bf16),
-            dma((2,)),
+            dma((4,)),
             dma((chunks, coils, slab)),
             dma((chunks, coils, slab)),
             dma((chunks, coils)),
@@ -287,7 +323,7 @@
             dma((coil,)),
         ],
         compiler_params=pltpu.CompilerParams(
-            collective_id=0, has_side_effects=True, vmem_limit_bytes=63 * 1024 * 1024
+            collective_id=0, has_side_effects=True, vmem_limit_bytes=VLIM * 1024 * 1024
         ),
     )(kspace, coil_maps, line_index, ky_table, kz_table)
 

time: 126 us -> 115 us (0.913)
  Pallas kernels: 123 us -> 113 us
    pallas_call x1, Pallas kernels: 123 us -> 113 us  [local(): pl.pallas_call(functools.partial(kernel, dims), out_shape=jax.ShapeDtypeS...]
where the time goes in v2:
time: 115 us
  Pallas kernels  113 us (98%)
  local copies, waits for them, and re-layouts  1.81 us (2%)
    pallas_call x1, Pallas kernels, local(): pl.pallas_call(functools.partial(kernel, dims), out_shape=jax.ShapeDtypeS...  113 us

profile of v2, /device:TPU:0, one launch (start us, length us, event | category | flops | bytes accessed | tf_op | source)
XLA Modules:
  0.0 114.8 jit_solution(2405005179841614386)
XLA Ops:
  0.0 0.0 copy-start
  0.0 0.8 copy-done
  0.8 113.0 %shard_map.55 = f32[8,2,48,384]{3,2,1,0:T(8,128)S(1)} custom-call(bf16[2,2,2,32,48,128]{5,4,3,2,1,0:T(8,128)(2,1)} %kspace_ref.1, bf16[2,2,32,48,384]{4,3,2,1,0:T(8,128)(2,1)} %maps_ref.1, s32[2,48,128]{2,1,0:T(8,128)S(1)} %copy-done, bf16[768,768]{1,0:T(8,128)(2,1)} %constant.8.ky_ref, bf16[768,768]{1,0:T(8,128)(2,1)} %constant.9.kz_ref), custom_call_target="tpu_custom_call" | custom-call | tf_op jit(solution)/shard_map/pallas_call | solution.py:301
  113.8 1.0 copy.7
Async XLA Ops:
  0.0 0.8 copy-start

commit v3 on v2

--- a/solution.py
+++ b/solution.py
@@ -36,7 +36,7 @@
 def kernel(
     dims,
     kspace_ref, maps_ref, index_ref, ky_ref, kz_ref, out_ref,
-    raw, samples, grid, maps, ky_tab, kz_tab, send, recv, image, part_send, part_recv,
+    raw, index, samples, grid, maps, ky_tab, kz_tab, send, recv, image, part_send, part_recv,
     in_sem, send_sem, recv_sem, own_sem, psend_sem, precv_sem,
 ):
     slab, coil, coils, offs, xr, kzb, kzp, lines, ny, yb, nz = dims
@@ -58,35 +58,52 @@
             barrier, inc=1, device_id={"coil": lax.rem(me_c + o, coil)}, device_id_type=MESH
         )
 
-    load_k = pltpu.make_async_copy(kspace_ref, raw, in_sem.at[0])
-    load_m = pltpu.make_async_copy(maps_ref, maps, in_sem.at[1])
-    load_y = pltpu.make_async_copy(ky_ref, ky_tab, in_sem.at[2])
-    load_z = pltpu.make_async_copy(kz_ref, kz_tab, in_sem.at[3])
-    for load in (load_k, load_y, load_m, load_z):
-        load.start()
+    def chunk_of(k):
+        return lax.rem(lax.div(me_c, owners) + 1 + k, chunks)
+
+    def load_k(k):
+        at = pl.ds(chunk_of(k) * slab, slab)
+        return pltpu.make_async_copy(
+            kspace_ref.at[:, :, :, at], raw.at[:, :, :, at], in_sem.at[3 + k]
+        )
+
+    load_i = pltpu.make_async_copy(index_ref, index, in_sem.at[3 + chunks])
+    load_i.start()
+    load_k(0).start()
+    load_m = pltpu.make_async_copy(maps_ref, maps, in_sem.at[0])
+    load_y = pltpu.make_async_copy(ky_ref, ky_tab, in_sem.at[1])
+    load_z = pltpu.make_async_copy(kz_ref, kz_tab, in_sem.at[2])
+    load_y.start()
+    for k in range(1, chunks):
+        load_k(k).start()
+    load_m.start()
+    load_z.start()
 
     if kzp != kzb:
         grid[...] = jnp.zeros_like(grid)
 
-    def unpack(first, i, carry):
+    count = min(ROWS, kzb)
+
+    def unpack(first, b, i, carry):
+        kz_at = pl.multiple_of(b * ROWS, ROWS)
         for c in range(coils):
             for t in range(offs):
                 angle = 2.0 * math.pi * t / PHASES
-                real = raw[0, c, t, first + i].astype(jnp.float32)
-                imag = raw[1, c, t, first + i].astype(jnp.float32)
+                real = raw[0, c, t, first + i, pl.ds(kz_at, count)].astype(jnp.float32)
+                imag = raw[1, c, t, first + i, pl.ds(kz_at, count)].astype(jnp.float32)
                 if t:
                     cosine, sine = math.cos(angle), math.sin(angle)
                     real, imag = cosine * real + sine * imag, cosine * imag - sine * real
                 for part, value in ((0, real), (1, imag)):
-                    at = pl.multiple_of(((part * coils + c) * slab + i) * kzs, 8)
-                    samples[t, pl.ds(at, kzb), :] = value
+                    at = pl.multiple_of(((part * coils + c) * slab + i) * kzs + kz_at, 8)
+                    samples[t, pl.ds(at, count), :] = value
         return carry
 
     ky_at = lax.broadcasted_iota(jnp.int32, (ny, offs * lines), 0)
 
     def place(first_kz, step, carry):
         kz = first_kz + step
-        picked = jnp.concatenate([index_ref[t, pl.ds(kz, 1), :] for t in range(offs)], axis=1)
+        picked = jnp.concatenate([index[t, pl.ds(kz, 1), :] for t in range(offs)], axis=1)
         hot = jnp.where(ky_at == picked, 1.0, 0.0).astype(jnp.bfloat16)
         left = jnp.concatenate(
             [samples[t, pl.ds(kz, rows, stride=kzs), :].astype(jnp.bfloat16) for t in range(offs)],
@@ -100,9 +117,6 @@
             grid[j, pl.ds(grid_at, rows), :] = placed[:, j * LANES : (j + 1) * LANES]
         return carry
 
-
-    def chunk_of(k):
-        return lax.rem(lax.div(me_c, owners) + 1 + k, chunks)
 
     def block_copy(k, c, o, kz_at):
         return pltpu.make_async_remote_copy(
@@ -168,6 +182,10 @@
                             lane >= p * yb - j * LANES, turned[(p - d) % slab][:, cut], tile
                         )
                     send[k, c, d, part, pl.ds(kz_at, ROWS), cut] = tile.astype(jnp.bfloat16)
+        @pl.when((k == 0) & (b == 0) & (c == 0))
+        def _():
+            pl.semaphore_wait(barrier, slab + coil - 2)
+
         for o in ORDER(slab):
             block_copy(k, c, o, kz_at).start()
 
@@ -179,18 +197,17 @@
 
     def chunk_pass(k, carry):
         first = chunk_of(k) * slab
-        lax.fori_loop(0, slab, functools.partial(unpack, first), 0)
+        load_k(k).wait()
 
         def block_pass(b, inner):
-            count = min(ROWS, kzb)
+            lax.fori_loop(0, slab, functools.partial(unpack, first, b), 0)
             lax.fori_loop(0, count, functools.partial(place, b * ROWS), 0, unroll=UNROLL)
             return lax.fori_loop(0, coils, functools.partial(rows_pass, k, b), inner)
 
         return lax.fori_loop(0, blocks, block_pass, carry)
 
-    load_k.wait()
+    load_i.wait()
     load_y.wait()
-    pl.semaphore_wait(barrier, slab + coil - 2)
     lax.fori_loop(0, chunks, chunk_pass, 0)
     load_m.wait()
     load_z.wait()
@@ -301,10 +318,11 @@
     return pl.pallas_call(
         functools.partial(kernel, dims),
         out_shape=jax.ShapeDtypeStruct((xo, 2, yb, nz), f32),
-        in_specs=[hbm, hbm, vmem, hbm, hbm],
+        in_specs=[hbm] * 5,
         out_specs=vmem,
         scratch_shapes=[
             pltpu.VMEM(kspace.shape, bf16),
+            pltpu.VMEM(line_index.shape, jnp.int32),
             pltpu.VMEM((offs, rows * up(kzb, 8), lines), f32),
             pltpu.VMEM((ny // LANES, kzp * rows, LANES), f32),
             pltpu.VMEM(coil_maps.shape, bf16),
@@ -315,7 +333,7 @@
             pltpu.VMEM((coils, ny, 2 * nz), f32),
             pltpu.VMEM((chunks, slab, 2, yb, nz), bf16),
             pltpu.VMEM((coil, xo, 2, yb, nz), bf16),
-            dma((4,)),
+            dma((4 + chunks,)),
             dma((chunks, coils, slab)),
             dma((chunks, coils, slab)),
             dma((chunks, coils)),

time: 115 us -> 114 us (level)
  no operation moved by 1% of the time
where the time goes in v3:
time: 114 us
  Pallas kernels  112 us (98%)
  local copies, waits for them, and re-layouts  1.81 us (2%)
    pallas_call x1, Pallas kernels, local(): pl.pallas_call(functools.partial(kernel, dims), out_shape=jax.ShapeDtypeS...  112 us

profile of v3, /device:TPU:0, one launch (start us, length us, event | category | flops | bytes accessed | tf_op | source)
XLA Modules:
  0.0 114.2 jit_solution(15728937069860065788)
XLA Ops:
  0.0 0.0 copy-start
  0.0 0.8 copy-done
  0.8 112.4 %shard_map.55 = f32[8,2,48,384]{3,2,1,0:T(8,128)S(1)} custom-call(bf16[2,2,2,32,48,128]{5,4,3,2,1,0:T(8,128)(2,1)} %kspace_ref.1, bf16[2,2,32,48,384]{4,3,2,1,0:T(8,128)(2,1)} %maps_ref.1, s32[2,48,128]{2,1,0:T(8,128)S(1)} %copy-done, bf16[768,768]{1,0:T(8,128)(2,1)} %constant.8.ky_ref, bf16[768,768]{1,0:T(8,128)(2,1)} %constant.9.kz_ref), custom_call_target="tpu_custom_call" | custom-call | tf_op jit(solution)/shard_map/pallas_call | solution.py:318
  113.2 1.0 copy.7
Async XLA Ops:
  0.0 0.8 copy-start
